TPU v7x, 128 devices: a whole 4x4x4 slice. The times are simulated.
128 devices in a mesh: row: 8 (over x, z_lo), col: 16 (over y, z_hi, core).
Axes of the slice: x: 4, y: 4, z: 4 (z_hi: 2, z_lo: 2; z = z_hi * 2 + z_lo), core: 2. Of those that a mesh axis runs over, the one named last changes fastest.
Arguments:
- tokens_in: bfloat16 [8192, 5120], P('row', 'col'), may hold values from -6 to 6
- token_grad: bfloat16 [8192, 5120], P('row', 'col'), may hold values from -6 to 6
- gate_gain: float32 [5120], replicated, may hold values from -4 to 4
- inner_weight: bfloat16 [5120, 13824], P(None, 'col'), may hold values from -0.078125 to 0.078125
- inner_bias: float32 [13824], P('col'), may hold values from -4 to 4
- outer_weight: bfloat16 [5120, 13824], P(None, 'col'), may hold values from -0.0546875 to 0.0546875
- inner_down: bfloat16 [5120, 64], replicated, may hold values from -0.078125 to 0.078125
- inner_up: bfloat16 [64, 13824], P(None, 'col'), may hold values from -0.1796875 to 0.1796875
- outer_down: bfloat16 [13824, 64], P('col'), may hold values from -0.0546875 to 0.0546875
- outer_up: bfloat16 [64, 5120], replicated, may hold values from -0.1796875 to 0.1796875
Outputs:
- tokens_grad: bfloat16 [8192, 5120], P('row', 'col')
- inner_down_grad: float32 [5120, 64], P('col')
- inner_up_grad: float32 [64, 13824], P(None, 'col')
- outer_down_grad: float32 [13824, 64], P('col')
- outer_up_grad: float32 [64, 5120], P(None, 'col')
All inputs are finite; a program needn't handle non-finite values.
Results may differ from a plain program's by a relative error of at most 0.023.
Values may be sent and summed in bfloat16 or wider, within the bound.
A program may use at most 128 MiB of HBM per device.

v0:
```python
import math
import jax
import jax.numpy as jnp
from jax import lax
from jax.sharding import PartitionSpec as P

SLOPE_SCALE = 0.7978845608028654
CUBIC = 0.044715


def gelu_value(pre):
    inner = SLOPE_SCALE * (pre + CUBIC * pre * pre * pre)
    return 0.5 * pre * (1.0 + jnp.tanh(inner))


def gelu_slope(pre):
    tangent = jnp.tanh(SLOPE_SCALE * (pre + CUBIC * pre * pre * pre))
    return 0.5 * (1.0 + tangent) + 0.5 * pre * (1.0 - tangent * tangent) * SLOPE_SCALE * (
        1.0 + 3.0 * CUBIC * pre * pre
    )


def plain_dot(left, right):
    return jnp.dot(left, right, preferred_element_type=jnp.float32)


def dot_rows(left, right):
    return lax.dot_general(
        left, right, (((1,), (1,)), ((), ())), preferred_element_type=jnp.float32
    )


def dot_cols(left, right):
    return lax.dot_general(
        left, right, (((0,), (0,)), ((), ())), preferred_element_type=jnp.float32
    )


def tree_sum(value, axis, size):
    step = 1
    while step < size:
        pairs = [(i, i ^ step) for i in range(size)]
        value = value + lax.ppermute(value, axis, pairs)
        step *= 2
    return value


def local(
    tokens_in,
    token_grad,
    gate_gain,
    inner_weight,
    inner_bias,
    outer_weight,
    inner_down,
    inner_up,
    outer_down,
    outer_up,
):
    n_col = lax.axis_size("col")
    n_row = lax.axis_size("row")
    col_index = lax.axis_index("col")
    local_width = token_grad.shape[1]
    tok_rows = tokens_in.shape[0]
    ff_local = inner_weight.shape[1]
    rank = inner_down.shape[1]
    gain_local = lax.dynamic_slice_in_dim(gate_gain, col_index * local_width, local_width, 0)
    gated_local = (gain_local[None, :] * token_grad.astype(jnp.float32)).astype(jnp.bfloat16)
    both_full = lax.all_gather(jnp.stack([tokens_in, gated_local]), "col", axis=2, tiled=True)
    tokens_full, gated_full = (both_full[0], both_full[1])
    inner_cat = jnp.concatenate([inner_weight, inner_down], axis=1)
    outer_cat = jnp.concatenate([outer_weight, outer_up.T], axis=1)
    forward_all = plain_dot(tokens_full, inner_cat)
    forward_sum = forward_all[:, :ff_local]
    inner_low = forward_all[:, ff_local:].astype(jnp.bfloat16)
    backward_all = plain_dot(gated_full, outer_cat)
    backward_sum = backward_all[:, :ff_local]
    grad_low = backward_all[:, ff_local:].astype(jnp.bfloat16)
    pre = forward_sum + plain_dot(inner_low, inner_up) + inner_bias[None, :]
    hidden = gelu_value(pre).astype(jnp.bfloat16)
    grad_hidden = backward_sum + dot_rows(grad_low, outer_down)
    grad_pre = (grad_hidden * gelu_slope(pre)).astype(jnp.bfloat16)
    pre_low_part = dot_rows(grad_pre, inner_up)
    block_part = dot_rows(grad_pre, inner_weight).astype(jnp.bfloat16).astype(jnp.float32)
    low_part = dot_rows(pre_low_part.astype(jnp.bfloat16), inner_down)
    tokens_grad = lax.psum_scatter(
        (block_part + low_part).astype(jnp.bfloat16), "col", scatter_dimension=1, tiled=True
    )
    hidden_low_part = plain_dot(hidden, outer_down)
    lows = tree_sum(jnp.concatenate([hidden_low_part, pre_low_part], axis=1), "col", n_col)
    hidden_low = lows[:, :rank].astype(jnp.bfloat16)
    pre_low = lows[:, rank:].astype(jnp.bfloat16)
    scale = 1.0 / math.sqrt(tok_rows * n_row)
    outer_down_term = dot_cols(hidden, grad_low)
    outer_up_term = dot_cols(gated_local, hidden_low)
    inner_down_term = dot_cols(tokens_in, pre_low)
    inner_up_term = dot_cols(grad_pre, inner_low)
    packed = jnp.concatenate(
        [outer_down_term, inner_up_term, outer_up_term, inner_down_term], axis=0
    )
    packed = tree_sum(packed, "row", n_row) * scale
    outer_down_grad = packed[:ff_local]
    inner_up_grad = packed[ff_local : 2 * ff_local].T
    outer_up_grad = packed[2 * ff_local : 2 * ff_local + local_width].T
    inner_down_grad = packed[2 * ff_local + local_width :]
    return (tokens_grad, inner_down_grad, inner_up_grad, outer_down_grad, outer_up_grad)


def solution(mesh):
    placed = (
        P("row", "col"),
        P("row", "col"),
        P(),
        P(None, "col"),
        P("col"),
        P(None, "col"),
        P(),
        P(None, "col"),
        P("col", None),
        P(),
    )
    return jax.shard_map(
        local,
        mesh=mesh,
        in_specs=placed,
        out_specs=(P("row", "col"), P("col", None), P(None, "col"), P("col", None), P(None, "col")),
        check_vma=False,
    )
```

profile of v0, /device:TPU:1, one launch (start us, length us, event | category | flops | bytes accessed | tf_op | source)
XLA Modules:
  0.0 329.9 jit_solution(954291616641102913)
XLA Ops:
  7.2 0.0 copy-start
  7.2 0.0 copy-start.3
  7.2 0.0 all-gather.2.cloned.1.call-start
  7.2 0.8 dynamic_slice.3
  8.1 1.3 fusion.17
  9.4 2.3 pad_maximum_fusion
  11.7 0.0 all-gather.2.cloned.1.call-update
  11.7 0.0 copy-start.9
  11.7 0.0 reduce-scatter.2.cloned.1.call-start
  11.7 133.4 %all-gather.2.cloned.1.call-done = bf16[2,1024,5120]{1,2,0:T(8,128)(2,1)} async-done(((bf16[2,1024,320]{1,2,0:T(8,128)(2,1)}), bf16[2,1024,5120]{1,2,0:T(8,128)(2,1)}) %all-gather.2.cloned.1.call-update) | async-done | bytes 20971536 | tf_op jit(solution)/shard_map/all_gather | solution.py:69
  145.2 0.0 copy-done.3
  145.2 15.8 %fusion = f32[1024,928]{0,1:T(8,128)S(1)} fusion(bf16[2,1024,5120]{1,2,0:T(8,128)(2,1)} %all-gather.2.cloned.1.call-done, bf16[5120,64]{0,1:T(8,128)(2,1)S(1)} %copy-done.3, bf16[5120,864]{0,1:T(8,128)(2,1)} %param.13), kind=kOutput, calls=%fused_computation.2 | convolution fusion | flops 9749790720 | bytes 23789568 | tf_op jit(solution)/shard_map/dot_general | solution.py:24
  161.0 0.0 copy-done
  161.0 0.0 copy-done.9
  161.0 0.0 copy-start.6
  161.0 0.0 copy-start.8
  161.0 4.0 %multiply_convert_fusion = (bf16[1024,864]{0,1:T(8,128)(2,1)}, f32[1024,864]{0,1:T(8,128)}) fusion(f32[864]{0:T(1024)S(1)} %copy-done.9, bf16[64,864]{1,0:T(8,128)(2,1)S(1)} %copy-done, f32[1024,928]{0,1:T(8,128)S(1)} %fusion), kind=kOutput, calls=%fused_computation.23 | convolution fusion | flops 123043840 | bytes 9223552 | tf_op jit(solution)/shard_map/dot_general | solution.py:24
  165.0 0.0 copy-done.6
  165.0 0.0 copy-done.8
  165.0 15.9 %fusion.1 = f32[1024,928]{0,1:T(8,128)S(1)} fusion(bf16[2,1024,5120]{1,2,0:T(8,128)(2,1)} %all-gather.2.cloned.1.call-done, bf16[5120,64]{0,1:T(8,128)(2,1)S(1)} %bitcast.29, bf16[5120,864]{0,1:T(8,128)(2,1)} %param.15), kind=kOutput, calls=%fused_computation.4 | convolution fusion | flops 9749790720 | bytes 23789568 | tf_op jit(solution)/shard_map/dot_general | solution.py:24
  180.9 0.0 copy-start.7
  180.9 0.0 copy-done.5
  180.9 5.5 %fusion.14 = bf16[1024,864]{0,1:T(8,128)(2,1)S(1)} fusion(f32[1024,864]{0,1:T(8,128)} %get-tuple-element.10, f32[1024,928]{0,1:T(8,128)S(1)} %fusion.1, bf16[864,64]{0,1:T(8,128)(2,1)S(1)} %copy-done.5), kind=kOutput, calls=%fused_computation.19 | convolution fusion | flops 131006464 | bytes 9220096 | tf_op jit(solution)/shard_map/dot_general | solution.py:28
  186.4 0.0 copy-done.7
  186.4 0.4 fusion.28
  186.9 13.7 %fusion.27 = bf16[1024,5120]{0,1:T(8,128)(2,1)S(1)} fusion(bf16[1024,864]{0,1:T(8,128)(2,1)S(1)} %fusion.14, bf16[5120,864]{0,1:T(8,128)(2,1)} %param.13), kind=kOutput, calls=%fused_computation.45 | convolution fusion | flops 9059696640 | bytes 21102592 | tf_op jit(solution)/shard_map/dot_general | solution.py:28
  200.6 6.8 %add_convert_fusion = bf16[1024,5120]{0,1:T(8,128)(2,1)} fusion(bf16[5120,64]{0,1:T(8,128)(2,1)} %param.16, bf16[1024,5120]{0,1:T(8,128)(2,1)S(1)} %fusion.27, f32[1024,64]{0,1:T(8,128)S(1)} %fusion.28), kind=kOutput, calls=%fused_computation | convolution fusion | flops 686882816 | bytes 21889024 | tf_op jit(solution)/shard_map/dot_general | solution.py:28
  207.4 0.0 reduce-scatter.2.cloned.1.call-update
  207.4 0.0 copy-start.1
  207.4 2.0 fusion.29
  209.5 0.3 collective-permute-start
  209.8 1.7 collective-permute-done
  211.5 0.1 fusion.25
  211.6 0.2 collective-permute-start.1
  211.7 14.7 %collective-permute-done.1 = f32[1024,128]{0,1:T(8,128)S(1)} collective-permute-done((f32[1024,128]{0,1:T(8,128)S(1)}, f32[1024,128]{0,1:T(8,128)S(1)}, u32[]{:S(2)}, u32[]{:S(2)}) %collective-permute-start.1) | collective-permute-done | bytes 524320 | tf_op jit(solution)/shard_map/ppermute | solution.py:43
  226.4 0.1 add.68
  226.5 0.0 copy-start.2
  226.5 0.1 collective-permute-start.2
  226.6 12.3 %collective-permute-done.2 = f32[1024,128]{0,1:T(8,128)S(1)} collective-permute-done((f32[1024,128]{0,1:T(8,128)S(1)}, f32[1024,128]{0,1:T(8,128)S(1)}, u32[]{:S(2)}, u32[]{:S(2)}) %collective-permute-start.2) | collective-permute-done | bytes 524320 | tf_op jit(solution)/shard_map/ppermute | solution.py:43
  238.9 0.1 add.69
  239.0 0.0 copy-start.4
  239.0 1.1 collective-permute-start.3
  240.2 0.0 copy-done.1
  240.2 1.6 fusion.21
  241.8 1.6 fusion.22
  243.4 14.5 %collective-permute-done.3 = f32[1024,128]{0,1:T(8,128)S(1)} collective-permute-done((f32[1024,128]{0,1:T(8,128)S(1)}, f32[1024,128]{0,1:T(8,128)S(1)}, u32[]{:S(2)}, u32[]{:S(2)}) %collective-permute-start.3) | collective-permute-done | bytes 524320 | tf_op jit(solution)/shard_map/ppermute | solution.py:43
  257.8 0.1 add_convert_fusion.1
  257.9 0.0 copy-done.2
  257.9 0.3 convolution_bitcast_fusion
  258.3 0.0 copy-done.4
  258.3 0.4 fusion.16
  258.7 0.2 concatenate.15
  258.9 0.1 collective-permute-start.4
  259.0 9.5 %collective-permute-done.4 = f32[2368,64]{0,1:T(8,128)S(1)} collective-permute-done((f32[2368,64]{0,1:T(8,128)S(1)}, f32[2368,64]{0,1:T(8,128)S(1)}, u32[]{:S(2)}, u32[]{:S(2)}) %collective-permute-start.4) | collective-permute-done | bytes 606240 | tf_op jit(solution)/shard_map/ppermute | solution.py:43
  268.5 0.1 add.71
  268.5 1.3 collective-permute-start.5
  269.8 8.3 %collective-permute-done.5 = f32[2368,64]{0,1:T(8,128)S(1)} collective-permute-done((f32[2368,64]{0,1:T(8,128)S(1)}, f32[2368,64]{0,1:T(8,128)S(1)}, u32[]{:S(2)}, u32[]{:S(2)}) %collective-permute-start.5) | collective-permute-done | bytes 606240 | tf_op jit(solution)/shard_map/ppermute | solution.py:43
  278.1 0.1 add.72
  278.2 2.6 collective-permute-start.6
  280.7 8.5 %collective-permute-done.6 = f32[2368,64]{0,1:T(8,128)S(1)} collective-permute-done((f32[2368,64]{0,1:T(8,128)S(1)}, f32[2368,64]{0,1:T(8,128)S(1)}, u32[]{:S(2)}, u32[]{:S(2)}) %collective-permute-start.6) | collective-permute-done | bytes 606240 | tf_op jit(solution)/shard_map/ppermute | solution.py:43
  289.2 0.1 add_multiply_fusion
  289.3 0.7 slice_bitcast_fusion.5
  290.0 0.8 fusion.26
  290.9 32.3 %reduce-scatter.2.cloned.1.call-done = bf16[1024,320]{0,1:T(8,128)(2,1)} async-done(((bf16[1024,5120]{0,1:T(8,128)(2,1)}), bf16[1024,320]{0,1:T(8,128)(2,1)}) %reduce-scatter.2.cloned.1.call-update) | async-done | bytes 655376 | tf_op jit(solution)/shard_map/reduce_scatter | solution.py:86
  (2 shorter events, 0.0 us)
Async XLA Ops:
  7.2 153.8 %copy-start = (bf16[64,864]{1,0:T(8,128)(2,1)S(1)}, bf16[64,864]{1,0:T(8,128)(2,1)}, u32[]{:S(2)}) copy-start(bf16[64,864]{1,0:T(8,128)(2,1)} %param.17) | copy-start | bytes 331780
  7.2 138.0 %copy-start.3 = (bf16[5120,64]{0,1:T(8,128)(2,1)S(1)}, bf16[5120,64]{0,1:T(8,128)(2,1)}, u32[]{:S(2)}) copy-start(bf16[5120,64]{0,1:T(8,128)(2,1)} %param.16) | copy-start | bytes 1966084
  7.2 138.0 %all-gather.2.cloned.1.call-start = ((), (), s32[]{:S(2)}) async-start(), calls=%async_computation.1 | async-start | bytes 22282240 | tf_op jit(solution)/shard_map/all_gather | solution.py:69
  11.7 149.3 %copy-start.9 = (f32[864]{0:T(1024)S(1)}, f32[864]{0:T(1024)}, u32[]{:S(2)}) copy-start(f32[864]{0:T(1024)} %param.14) | copy-start | bytes 10372
  11.7 311.4 %reduce-scatter.2.cloned.1.call-start = ((), (), s32[]{:S(2)}) async-start(), calls=%async_computation.2 | async-start | bytes 11141120 | tf_op jit(solution)/shard_map/reduce_scatter | solution.py:86
  161.0 4.0 %copy-start.6 = (f32[1024,928]{0,1:T(8,128)}, f32[1024,928]{0,1:T(8,128)S(1)}, u32[]{:S(2)}) copy-start(f32[1024,928]{0,1:T(8,128)S(1)} %fusion) | copy-start | bytes 11403268
  161.0 4.0 %copy-start.8 = (bf16[64,5120]{1,0:T(8,128)(2,1)S(1)}, bf16[64,5120]{1,0:T(8,128)(2,1)}, u32[]{:S(2)}) copy-start(bf16[64,5120]{1,0:T(8,128)(2,1)} %param.19) | copy-start | bytes 1966084
  165.0 15.9 %copy-start.5 = (bf16[864,64]{0,1:T(8,128)(2,1)S(1)}, bf16[864,64]{0,1:T(8,128)(2,1)}, u32[]{:S(2)}) copy-start(bf16[864,64]{0,1:T(8,128)(2,1)} %param.18) | copy-start | bytes 331780
  180.9 5.5 %copy-start.7 = (f32[1024,928]{0,1:T(8,128)}, f32[1024,928]{0,1:T(8,128)S(1)}, u32[]{:S(2)}) copy-start(f32[1024,928]{0,1:T(8,128)S(1)} %fusion.1) | copy-start | bytes 11403268
  207.4 32.8 %copy-start.1 = (bf16[1024,864]{0,1:T(8,128)(2,1)S(1)}, bf16[1024,864]{0,1:T(8,128)(2,1)}, u32[]{:S(2)}) copy-start(bf16[1024,864]{0,1:T(8,128)(2,1)} %get-tuple-element.9) | copy-start | bytes 5308420
  209.5 2.0 collective-permute-start
  211.6 14.9 %collective-permute-start.1 = (f32[1024,128]{0,1:T(8,128)S(1)}, f32[1024,128]{0,1:T(8,128)S(1)}, u32[]{:S(2)}, u32[]{:S(2)}) collective-permute-start(f32[1024,128]{0,1:T(8,128)S(1)} %fusion.25), channel_id=1, source_target_pairs={{0,2},{1,3},{2,0},{3,1},{4,6},{5,7},{6,4},{7,5},{8,10},{9,11},{10,... | collective-permute-start | bytes 1572872 | tf_op jit(solution)/shard_map/ppermute | solution.py:43
  226.5 31.4 %copy-start.2 = (bf16[1024,320]{0,1:T(8,128)(2,1)S(1)}, bf16[1024,320]{0,1:T(8,128)(2,1)}, u32[]{:S(2)}) copy-start(bf16[1024,320]{0,1:T(8,128)(2,1)} %param.10) | copy-start | bytes 1966084
  226.5 12.4 %collective-permute-start.2 = (f32[1024,128]{0,1:T(8,128)S(1)}, f32[1024,128]{0,1:T(8,128)S(1)}, u32[]{:S(2)}, u32[]{:S(2)}) collective-permute-start(f32[1024,128]{0,1:T(8,128)S(1)} %add.68), channel_id=1, source_target_pairs={{0,4},{1,5},{2,6},{3,7},{4,0},{5,1},{6,2},{7,3},{8,12},{9,13},{10,... | collective-permute-start | bytes 1572872 | tf_op jit(solution)/shard_map/ppermute | solution.py:43
  239.0 19.2 %copy-start.4 = (bf16[1024,320]{0,1:T(8,128)(2,1)S(1)}, bf16[1024,320]{0,1:T(8,128)(2,1)}, u32[]{:S(2)}) copy-start(bf16[1024,320]{0,1:T(8,128)(2,1)} %param.11) | copy-start | bytes 1966084
  239.0 18.8 %collective-permute-start.3 = (f32[1024,128]{0,1:T(8,128)S(1)}, f32[1024,128]{0,1:T(8,128)S(1)}, u32[]{:S(2)}, u32[]{:S(2)}) collective-permute-start(f32[1024,128]{0,1:T(8,128)S(1)} %add.69), channel_id=1, source_target_pairs={{0,8},{1,9},{2,10},{3,11},{4,12},{5,13},{6,14},{7,15},{8,0},{9,1},... | collective-permute-start | bytes 1572872 | tf_op jit(solution)/shard_map/ppermute | solution.py:43
  258.9 9.6 %collective-permute-start.4 = (f32[2368,64]{0,1:T(8,128)S(1)}, f32[2368,64]{0,1:T(8,128)S(1)}, u32[]{:S(2)}, u32[]{:S(2)}) collective-permute-start(f32[2368,64]{0,1:T(8,128)S(1)} %concatenate.15), channel_id=1, source_target_pairs={{0,16},{16,0},{32,48},{48,32},{64,80},{80,64},{96,112},{112,96},{1... | collective-permute-start | bytes 1818632 | tf_op jit(solution)/shard_map/ppermute | solution.py:43
  268.5 9.6 %collective-permute-start.5 = (f32[2368,64]{0,1:T(8,128)S(1)}, f32[2368,64]{0,1:T(8,128)S(1)}, u32[]{:S(2)}, u32[]{:S(2)}) collective-permute-start(f32[2368,64]{0,1:T(8,128)S(1)} %add.71), channel_id=1, source_target_pairs={{0,32},{16,48},{32,0},{48,16},{64,96},{80,112},{96,64},{112,80},{1... | collective-permute-start | bytes 1818632 | tf_op jit(solution)/shard_map/ppermute | solution.py:43
  278.2 11.1 %collective-permute-start.6 = (f32[2368,64]{0,1:T(8,128)S(1)}, f32[2368,64]{0,1:T(8,128)S(1)}, u32[]{:S(2)}, u32[]{:S(2)}) collective-permute-start(f32[2368,64]{0,1:T(8,128)S(1)} %add.72), channel_id=1, source_target_pairs={{0,64},{16,80},{32,96},{48,112},{64,0},{80,16},{96,32},{112,48},{1... | collective-permute-start | bytes 1818632 | tf_op jit(solution)/shard_map/ppermute | solution.py:43
Sparse Core Ops, SparseCore 0:
  11.8 133.3 all-gather.1
  207.5 115.5 reduce-scatter.1
where the time goes:
time: 330 us
  waiting for transfers between devices  235 us (71%)
  matrix products  68.1 us (21%)
  between operations  14.3 us (4%)
  starting transfers between devices  5.78 us (2%)
  other arithmetic  4.07 us (1%)
    all_gather x1, waiting for transfers between devices, local(): lax.all_gather(jnp.stack([tokens_in, gated_local]), 'col', axis=2, tiled=...  133 us
    ppermute x7, waiting for transfers between devices, tree_sum(): value = value + lax.ppermute(value, axis, pairs)  69.3 us
    dot_general x4, matrix products, plain_dot(): return jnp.dot(left, right, preferred_element_type=jnp.float32)  37.7 us
    reduce_scatter x1, waiting for transfers between devices, local(): lax.psum_scatter((block_part + low_part).astype(jnp.bfloat16), 'col', sca...  32.3 us
    dot_general x4, matrix products, dot_rows(): lax.dot_general(left, right, (((1,), (1,)), ((), ())), preferred_element_...  26.4 us
  transfers between devices with their start and end apart: 9, of which 9 were waited for; matrix products, arithmetic and copies ran while one was open for 3% of the time, Pallas kernels for 0%

commit v1 on v0

--- a/solution.py
+++ b/solution.py
@@ -3,6 +3,7 @@
 import jax.numpy as jnp
 from jax import lax
 from jax.sharding import PartitionSpec as P
+from jax.lax import all_to_all, psum
 
 SLOPE_SCALE = 0.7978845608028654
 CUBIC = 0.044715
@@ -66,7 +67,15 @@
     rank = inner_down.shape[1]
     gain_local = lax.dynamic_slice_in_dim(gate_gain, col_index * local_width, local_width, 0)
     gated_local = (gain_local[None, :] * token_grad.astype(jnp.float32)).astype(jnp.bfloat16)
-    both_full = lax.all_gather(jnp.stack([tokens_in, gated_local]), "col", axis=2, tiled=True)
+    both_full = jnp.concatenate(
+        all_to_all(
+            jnp.stack(psum(1, "col") * [jnp.stack([tokens_in, gated_local])]),
+            "col",
+            split_axis=0,
+            concat_axis=0,
+        ),
+        2,
+    )
     tokens_full, gated_full = (both_full[0], both_full[1])
     inner_cat = jnp.concatenate([inner_weight, inner_down], axis=1)
     outer_cat = jnp.concatenate([outer_weight, outer_up.T], axis=1)

time: 330 us -> 453 us (1.37)
  blocking collectives: 0 us -> 239 us
  waiting for transfers between devices: 235 us -> 100 us
  local copies, waits for them, and re-layouts: 2.66 us -> 21.8 us
    all_to_all x0 -> x1, blocking collectives: none -> 239 us  [local(): all_to_all(jnp.stack(psum(1, 'col') * [jnp.stack([tokens_in, gated_local]...]
    all_gather x1 -> x0, waiting for transfers between devices: 133 us -> none  [local(): lax.all_gather(jnp.stack([tokens_in, gated_local]), 'col', axis=2, tiled=...]
    all_to_all x0 -> x1, local copies, waits for them, and re-layouts: none -> 10.3 us  [local(): all_to_all(jnp.stack(psum(1, 'col') * [jnp.stack([tokens_in, gated_local]...]
    slice x0 -> x1, local copies, waits for them, and re-layouts: none -> 6.19 us  [local(): tokens_full, gated_full = (both_full[0], both_full[1])]
    reduce_scatter x1, waiting for transfers between devices: 32.3 us -> 26.6 us  [local(): lax.psum_scatter((block_part + low_part).astype(jnp.bfloat16), 'col', sca...]
  transfers between devices with their start and end apart: 9 -> 8, of which waited for: 9 -> 8; matrix products, arithmetic and copies ran while one was open for 3% -> 2% of each run, Pallas kernels for 0% -> 0%
where the time goes in v1:
time: 453 us
  blocking collectives  239 us (53%)
  waiting for transfers between devices  100 us (22%)
  matrix products  67.1 us (15%)
  local copies, waits for them, and re-layouts  21.8 us (5%)
  between operations  14.3 us (3%)
  starting transfers between devices  7.44 us (2%)
    all_to_all x1, blocking collectives, local(): all_to_all(jnp.stack(psum(1, 'col') * [jnp.stack([tokens_in, gated_local]...  239 us
    ppermute x7, waiting for transfers between devices, tree_sum(): value = value + lax.ppermute(value, axis, pairs)  73.4 us
    dot_general x4, matrix products, plain_dot(): return jnp.dot(left, right, preferred_element_type=jnp.float32)  37.8 us
    reduce_scatter x1, waiting for transfers between devices, local(): lax.psum_scatter((block_part + low_part).astype(jnp.bfloat16), 'col', sca...  26.6 us
    dot_general x4, matrix products, dot_rows(): lax.dot_general(left, right, (((1,), (1,)), ((), ())), preferred_element_...  25.4 us
    all_to_all x1, local copies, waits for them, and re-layouts, local(): all_to_all(jnp.stack(psum(1, 'col') * [jnp.stack([tokens_in, gated_local]...  10.3 us
  transfers between devices with their start and end apart: 8, of which 8 were waited for; matrix products, arithmetic and copies ran while one was open for 2% of the time, Pallas kernels for 0%

profile of v1, /device:TPU:1, one launch (start us, length us, event | category | flops | bytes accessed | tf_op | source)
XLA Modules:
  0.0 453.0 jit_solution(2842672419000578386)
XLA Ops:
  7.2 0.0 copy-start
  7.2 0.0 reduce-scatter.2.cloned.1.call-start
  7.2 0.8 dynamic_slice.3
  8.0 0.0 copy-start.6
  8.0 1.3 fusion.17
  9.3 0.0 copy-done.6
  9.3 1.2 pad_maximum_fusion
  10.5 2.7 stack.11
  13.2 239.4 %all_to_all.5 = bf16[16,2,1024,320]{2,3,1,0:T(8,128)(2,1)} all-to-all(bf16[16,2,1024,320]{2,3,1,0:T(8,128)(2,1)S(1)} %stack.11), channel_id=1, replica_groups=mesh['row'=8,'col'=16] {'col'}, dimensions={0} | all-to-all | bytes 41943040 | tf_op jit(solution)/shard_map/all_to_all | solution.py:71
  252.6 10.3 %copy.18 = bf16[16,2,1024,320]{2,3,0,1:T(8,128)(2,1)S(1)} copy(bf16[16,2,1024,320]{2,3,1,0:T(8,128)(2,1)} %all_to_all.5) | data formatting | bytes 41943040 | tf_op jit(solution)/shard_map/all_to_all | solution.py:71
  262.9 0.0 copy-start.8
  262.9 6.2 %fusion.26 = (bf16[1,1024,16,320]{1,3,2,0:T(8,128)(2,1)}, bf16[1,1024,16,320]{1,3,2,0:T(8,128)(2,1)S(1)}) fusion(bf16[2,1024,16,320]{1,3,2,0:T(8,128)(2,1)S(1)} %bitcast.29), kind=kLoop, calls=%fused_computation.43 | loop fusion | bytes 41943040 | tf_op jit(solution)/shard_map/slice | solution.py:79
  269.1 0.0 copy-done.8
  269.1 0.0 copy-start.3
  269.1 16.6 %fusion = f32[1024,928]{0,1:T(8,128)} fusion(bf16[1024,5120]{0,1:T(8,128)(2,1)} %bitcast.31, bf16[5120,64]{0,1:T(8,128)(2,1)S(1)} %bitcast.33, bf16[5120,864]{0,1:T(8,128)(2,1)} %param.15), kind=kOutput, calls=%fused_computation.2 | convolution fusion | flops 9749790720 | bytes 23789568 | tf_op jit(solution)/shard_map/dot_general | solution.py:25
  285.7 0.0 copy-done.3
  285.7 14.2 %fusion.4 = f32[1024,928]{0,1:T(8,128)} fusion(bf16[1024,5120]{0,1:T(8,128)(2,1)S(1)} %bitcast.30, bf16[5120,64]{0,1:T(8,128)(2,1)S(1)} %copy-done.3, bf16[5120,864]{0,1:T(8,128)(2,1)} %param.13), kind=kOutput, calls=%fused_computation.6 | convolution fusion | flops 9749790720 | bytes 23789568 | tf_op jit(solution)/shard_map/dot_general | solution.py:25
  300.0 0.0 copy-done
  300.0 0.0 copy-done.9
  300.0 4.9 %multiply_convert_fusion = (bf16[1024,864]{0,1:T(8,128)(2,1)}, f32[1024,864]{0,1:T(8,128)S(1)}) fusion(f32[864]{0:T(1024)S(1)} %copy-done.9, bf16[64,864]{1,0:T(8,128)(2,1)S(1)} %copy-done, f32[1024,928]{0,1:T(8,128)} %fusion.4), kind=kOutput, calls=%fused_computation.22 | convolution fusion | flops 123043840 | bytes 9223552 | tf_op jit(solution)/shard_map/dot_general | solution.py:25
  304.9 0.0 copy-done.5
  304.9 4.6 %fusion.14 = bf16[1024,864]{0,1:T(8,128)(2,1)S(1)} fusion(f32[1024,864]{0,1:T(8,128)S(1)} %get-tuple-element.12, f32[1024,928]{0,1:T(8,128)} %fusion, bf16[864,64]{0,1:T(8,128)(2,1)S(1)} %copy-done.5), kind=kOutput, calls=%fused_computation.18 | convolution fusion | flops 131006464 | bytes 9220096 | tf_op jit(solution)/shard_map/dot_general | solution.py:29
  309.5 0.4 fusion.29
  310.0 13.6 %fusion.28 = bf16[1024,5120]{0,1:T(8,128)(2,1)S(1)} fusion(bf16[1024,864]{0,1:T(8,128)(2,1)S(1)} %fusion.14, bf16[5120,864]{0,1:T(8,128)(2,1)} %param.13), kind=kOutput, calls=%fused_computation.45 | convolution fusion | flops 9059696640 | bytes 21102592 | tf_op jit(solution)/shard_map/dot_general | solution.py:29
  323.5 6.8 %add_convert_fusion = bf16[1024,5120]{0,1:T(8,128)(2,1)} fusion(bf16[5120,64]{0,1:T(8,128)(2,1)} %param.16, bf16[1024,5120]{0,1:T(8,128)(2,1)S(1)} %fusion.28, f32[1024,64]{0,1:T(8,128)S(1)} %fusion.29), kind=kOutput, calls=%fused_computation.1 | convolution fusion | flops 686882816 | bytes 21889024 | tf_op jit(solution)/shard_map/dot_general | solution.py:29
  330.3 0.0 reduce-scatter.2.cloned.1.call-update
  330.3 0.0 copy-start.1
  330.3 2.0 fusion.30
  332.4 1.6 collective-permute-start
  334.1 1.5 collective-permute-done
  335.6 0.1 fusion.25
  335.7 0.3 collective-permute-start.1
  336.0 14.4 %collective-permute-done.1 = f32[1024,128]{0,1:T(8,128)S(1)} collective-permute-done((f32[1024,128]{0,1:T(8,128)S(1)}, f32[1024,128]{0,1:T(8,128)S(1)}, u32[]{:S(2)}, u32[]{:S(2)}) %collective-permute-start.1) | collective-permute-done | bytes 524320 | tf_op jit(solution)/shard_map/ppermute | solution.py:44
  350.4 0.1 add.68
  350.5 0.0 copy-start.2
  350.5 0.1 collective-permute-start.2
  350.6 12.2 %collective-permute-done.2 = f32[1024,128]{0,1:T(8,128)S(1)} collective-permute-done((f32[1024,128]{0,1:T(8,128)S(1)}, f32[1024,128]{0,1:T(8,128)S(1)}, u32[]{:S(2)}, u32[]{:S(2)}) %collective-permute-start.2) | collective-permute-done | bytes 524320 | tf_op jit(solution)/shard_map/ppermute | solution.py:44
  362.8 0.1 add.69
  362.9 0.0 copy-start.4
  362.9 0.0 copy-start.7
  362.9 1.3 collective-permute-start.3
  364.1 0.0 copy-done.1
  364.1 1.6 fusion.21
  365.7 1.6 fusion.22
  367.4 11.6 %collective-permute-done.3 = f32[1024,128]{0,1:T(8,128)S(1)} collective-permute-done((f32[1024,128]{0,1:T(8,128)S(1)}, f32[1024,128]{0,1:T(8,128)S(1)}, u32[]{:S(2)}, u32[]{:S(2)}) %collective-permute-start.3) | collective-permute-done | bytes 524320 | tf_op jit(solution)/shard_map/ppermute | solution.py:44
  378.9 0.1 add_convert_fusion.1
  379.0 0.0 copy-done.2
  379.0 0.3 convolution_bitcast_fusion
  379.4 0.0 copy-done.4
  379.4 0.0 copy-done.7
  379.4 0.4 fusion.16
  379.8 0.2 concatenate.15
  380.0 0.2 collective-permute-start.4
  380.2 12.0 %collective-permute-done.4 = f32[2368,64]{0,1:T(8,128)S(1)} collective-permute-done((f32[2368,64]{0,1:T(8,128)S(1)}, f32[2368,64]{0,1:T(8,128)S(1)}, u32[]{:S(2)}, u32[]{:S(2)}) %collective-permute-start.4) | collective-permute-done | bytes 606240 | tf_op jit(solution)/shard_map/ppermute | solution.py:44
  392.1 0.1 add.71
  392.2 1.2 collective-permute-start.5
  393.5 8.3 %collective-permute-done.5 = f32[2368,64]{0,1:T(8,128)S(1)} collective-permute-done((f32[2368,64]{0,1:T(8,128)S(1)}, f32[2368,64]{0,1:T(8,128)S(1)}, u32[]{:S(2)}, u32[]{:S(2)}) %collective-permute-start.5) | collective-permute-done | bytes 606240 | tf_op jit(solution)/shard_map/ppermute | solution.py:44
  401.8 0.1 add.72
  401.8 2.7 collective-permute-start.6
  404.5 13.4 %collective-permute-done.6 = f32[2368,64]{0,1:T(8,128)S(1)} collective-permute-done((f32[2368,64]{0,1:T(8,128)S(1)}, f32[2368,64]{0,1:T(8,128)S(1)}, u32[]{:S(2)}, u32[]{:S(2)}) %collective-permute-start.6) | collective-permute-done | bytes 606240 | tf_op jit(solution)/shard_map/ppermute | solution.py:44
  417.9 0.1 add_multiply_fusion
  418.0 0.7 slice_bitcast_fusion.1
  418.8 0.8 fusion.27
  419.6 26.6 %reduce-scatter.2.cloned.1.call-done = bf16[1024,320]{0,1:T(8,128)(2,1)} async-done(((bf16[1024,5120]{0,1:T(8,128)(2,1)}), bf16[1024,320]{0,1:T(8,128)(2,1)}) %reduce-scatter.2.cloned.1.call-update) | async-done | bytes 655376 | tf_op jit(solution)/shard_map/reduce_scatter | solution.py:95
  (3 shorter events, 0.0 us)
Async XLA Ops:
  7.2 292.8 %copy-start = (bf16[64,864]{1,0:T(8,128)(2,1)S(1)}, bf16[64,864]{1,0:T(8,128)(2,1)}, u32[]{:S(2)}) copy-start(bf16[64,864]{1,0:T(8,128)(2,1)} %param.17) | copy-start | bytes 331780
  7.2 439.0 %reduce-scatter.2.cloned.1.call-start = ((), (), s32[]{:S(2)}) async-start(), calls=%async_computation.2 | async-start | bytes 11141120 | tf_op jit(solution)/shard_map/reduce_scatter | solution.py:95
  8.0 1.3 copy-start.6
  262.9 6.2 %copy-start.8 = (bf16[64,5120]{1,0:T(8,128)(2,1)S(1)}, bf16[64,5120]{1,0:T(8,128)(2,1)}, u32[]{:S(2)}) copy-start(bf16[64,5120]{1,0:T(8,128)(2,1)} %param.19) | copy-start | bytes 1966084
  269.1 16.6 %copy-start.3 = (bf16[5120,64]{0,1:T(8,128)(2,1)S(1)}, bf16[5120,64]{0,1:T(8,128)(2,1)}, u32[]{:S(2)}) copy-start(bf16[5120,64]{0,1:T(8,128)(2,1)} %param.16) | copy-start | bytes 1966084
  285.7 14.2 %copy-start.9 = (f32[864]{0:T(1024)S(1)}, f32[864]{0:T(1024)}, u32[]{:S(2)}) copy-start(f32[864]{0:T(1024)} %param.14) | copy-start | bytes 10372
  300.0 4.9 %copy-start.5 = (bf16[864,64]{0,1:T(8,128)(2,1)S(1)}, bf16[864,64]{0,1:T(8,128)(2,1)}, u32[]{:S(2)}) copy-start(bf16[864,64]{0,1:T(8,128)(2,1)} %param.18) | copy-start | bytes 331780
  330.3 33.8 %copy-start.1 = (bf16[1024,864]{0,1:T(8,128)(2,1)S(1)}, bf16[1024,864]{0,1:T(8,128)(2,1)}, u32[]{:S(2)}) copy-start(bf16[1024,864]{0,1:T(8,128)(2,1)} %get-tuple-element.11) | copy-start | bytes 5308420
  332.4 3.2 collective-permute-start
  335.7 14.7 %collective-permute-start.1 = (f32[1024,128]{0,1:T(8,128)S(1)}, f32[1024,128]{0,1:T(8,128)S(1)}, u32[]{:S(2)}, u32[]{:S(2)}) collective-permute-start(f32[1024,128]{0,1:T(8,128)S(1)} %fusion.25), channel_id=1, source_target_pairs={{0,2},{1,3},{2,0},{3,1},{4,6},{5,7},{6,4},{7,5},{8,10},{9,11},{10,... | collective-permute-start | bytes 1572872 | tf_op jit(solution)/shard_map/ppermute | solution.py:44
  350.5 28.5 %copy-start.2 = (bf16[1024,320]{0,1:T(8,128)(2,1)S(1)}, bf16[1024,320]{0,1:T(8,128)(2,1)}, u32[]{:S(2)}) copy-start(bf16[1024,320]{0,1:T(8,128)(2,1)} %param.10) | copy-start | bytes 1966084
  350.5 12.3 %collective-permute-start.2 = (f32[1024,128]{0,1:T(8,128)S(1)}, f32[1024,128]{0,1:T(8,128)S(1)}, u32[]{:S(2)}, u32[]{:S(2)}) collective-permute-start(f32[1024,128]{0,1:T(8,128)S(1)} %add.68), channel_id=1, source_target_pairs={{0,4},{1,5},{2,6},{3,7},{4,0},{5,1},{6,2},{7,3},{8,12},{9,13},{10,... | collective-permute-start | bytes 1572872 | tf_op jit(solution)/shard_map/ppermute | solution.py:44
  362.9 16.5 %copy-start.4 = (bf16[1024,320]{0,1:T(8,128)(2,1)S(1)}, bf16[1024,320]{0,1:T(8,128)(2,1)}, u32[]{:S(2)}) copy-start(bf16[1024,320]{0,1:T(8,128)(2,1)} %param.11) | copy-start | bytes 1966084
  362.9 16.5 %copy-start.7 = (f32[320]{0:T(512)S(1)}, f32[320]{0:T(512)}, u32[]{:S(2)}) copy-start(f32[320]{0:T(512)} %copy-done.6) | copy-start | bytes 3844
  362.9 16.0 %collective-permute-start.3 = (f32[1024,128]{0,1:T(8,128)S(1)}, f32[1024,128]{0,1:T(8,128)S(1)}, u32[]{:S(2)}, u32[]{:S(2)}) collective-permute-start(f32[1024,128]{0,1:T(8,128)S(1)} %add.69), channel_id=1, source_target_pairs={{0,8},{1,9},{2,10},{3,11},{4,12},{5,13},{6,14},{7,15},{8,0},{9,1},... | collective-permute-start | bytes 1572872 | tf_op jit(solution)/shard_map/ppermute | solution.py:44
  380.0 12.1 %collective-permute-start.4 = (f32[2368,64]{0,1:T(8,128)S(1)}, f32[2368,64]{0,1:T(8,128)S(1)}, u32[]{:S(2)}, u32[]{:S(2)}) collective-permute-start(f32[2368,64]{0,1:T(8,128)S(1)} %concatenate.15), channel_id=1, source_target_pairs={{0,16},{16,0},{32,48},{48,32},{64,80},{80,64},{96,112},{112,96},{1... | collective-permute-start | bytes 1818632 | tf_op jit(solution)/shard_map/ppermute | solution.py:44
  392.2 9.6 %collective-permute-start.5 = (f32[2368,64]{0,1:T(8,128)S(1)}, f32[2368,64]{0,1:T(8,128)S(1)}, u32[]{:S(2)}, u32[]{:S(2)}) collective-permute-start(f32[2368,64]{0,1:T(8,128)S(1)} %add.71), channel_id=1, source_target_pairs={{0,32},{16,48},{32,0},{48,16},{64,96},{80,112},{96,64},{112,80},{1... | collective-permute-start | bytes 1818632 | tf_op jit(solution)/shard_map/ppermute | solution.py:44
  401.8 16.1 %collective-permute-start.6 = (f32[2368,64]{0,1:T(8,128)S(1)}, f32[2368,64]{0,1:T(8,128)S(1)}, u32[]{:S(2)}, u32[]{:S(2)}) collective-permute-start(f32[2368,64]{0,1:T(8,128)S(1)} %add.72), channel_id=1, source_target_pairs={{0,64},{16,80},{32,96},{48,112},{64,0},{80,16},{96,32},{112,48},{1... | collective-permute-start | bytes 1818632 | tf_op jit(solution)/shard_map/ppermute | solution.py:44
Sparse Core Ops, SparseCore 0:
  330.5 115.6 reduce-scatter.1
